TPU v7x, 32 devices: a whole 2x2x4 slice. The times are simulated.
32 devices in a mesh: corpus: 4 (over y, x), fsdp: 8 (over z, core).
Axes of the slice: x: 2, y: 2, z: 4, core: 2. Of those that a mesh axis runs over, the one named last changes fastest.
Arguments:
- inputs: bfloat16 [2048, 4096], P('fsdp', 'corpus'), may hold values from -128 to 128
- norm_gain: float32 [4096], replicated, may hold values from 0.1 to 1.9
- w_query: bfloat16 [4096, 8192], P('fsdp', 'corpus'), may hold values from -0.09375 to 0.09375
- w_key: bfloat16 [4096, 1024], P('fsdp', 'corpus'), may hold values from -0.09375 to 0.09375
- w_value: bfloat16 [4096, 1024], P('fsdp', 'corpus'), may hold values from -0.375 to 0.375
- query_bias: float32 [8192], P('corpus'), may hold values from -16 to 16
- key_bias: float32 [1024], P('corpus'), may hold values from -16 to 16
- value_bias: float32 [1024], P('corpus'), may hold values from -4 to 4
- key_cache: bfloat16 [8, 2048, 1024], P('fsdp', None, 'corpus'), may hold values from -16 to 16
- value_cache: bfloat16 [8, 2048, 1024], P('fsdp', None, 'corpus'), may hold values from -16 to 16
- source_doc: int32 [32], P('fsdp'), may hold values from 0 to 7, as said below
- prefix_len: int32 [32], P('fsdp'), may hold values from 1 to 2048
Outputs:
- attention: bfloat16 [2048, 8192], P('fsdp', 'corpus')
Inputs may be any that keep to these rules, and one draw needn't show every extreme that they name: `source_doc`: within the suffixes of one index of fsdp (aligned blocks of 4) no document appears more than 2 times, and one document, drawn from the seed, appears exactly 2 times in every such block.
All inputs are finite; a program needn't handle non-finite values.
Results may differ from a plain program's by a relative error of at most 0.0075.
The roundings to bfloat16 on the way count: a program that leaves them out, or rounds other values in their place, can miss the bound.
Values may be sent and summed in bfloat16 or wider, within the bound.
A program may use at most 128 MiB of HBM per device.

v0:
```python
import jax
import jax.numpy as jnp
from jax import lax
from jax.sharding import PartitionSpec as P

HD = 128
SL = 64
CAP = 2
EPS = 1e-06
THETA = 1000000.0
MASKED = -1e30


def rope_tables(position, width):
    half = width // 2
    freq = THETA ** (-(jnp.arange(half, dtype=jnp.float32) * 2.0 / width))
    angle = position.astype(jnp.float32)[..., None] * freq
    angle = jnp.concatenate([angle, angle], axis=-1)
    return (jnp.cos(angle), jnp.sin(angle))


def rotate(vector, cosine, sine):
    half = vector.shape[-1] // 2
    turned = jnp.concatenate([-vector[..., half:], vector[..., :half]], axis=-1)
    return vector * cosine + turned * sine


def normalize(rows, norm_gain):
    wide = rows.astype(jnp.float32)
    spread = jnp.mean(wide * wide, axis=-1, keepdims=True)
    return (wide * lax.rsqrt(spread + EPS) * norm_gain).astype(jnp.bfloat16)


def partial_attend(query, keys, values, live):
    count = query.shape[0]
    width = query.shape[2]
    length = keys.shape[0]
    kv_heads = keys.shape[1] // width
    group = query.shape[1] // kv_heads
    grouped = query.reshape(count, kv_heads, group, width)
    key_rows = keys.reshape(length, kv_heads, width)
    scores = jnp.einsum(
        "tkgd,lkd->tkgl", grouped, key_rows, preferred_element_type=jnp.float32
    ) * width ** (-0.5)
    scores = jnp.where(live[:, None, None, :], scores, MASKED)
    peak = jnp.max(scores, axis=-1)
    weights = jnp.exp(scores - peak[..., None])
    total = jnp.sum(weights, axis=-1)
    rounded = weights.astype(jnp.bfloat16)
    value_rows = values.reshape(length, kv_heads, width)
    weighted = jnp.einsum("tkgl,lkd->tkgd", rounded, value_rows, preferred_element_type=jnp.float32)
    return (
        weighted.reshape(count, kv_heads * group * width),
        peak.reshape(count, kv_heads * group),
        total.reshape(count, kv_heads * group),
    )


def settle(part):
    weighted, peak, total = part
    shape = peak.shape + (-1,)
    normed = (
        (weighted.reshape(shape) / total[..., None]).reshape(weighted.shape).astype(jnp.bfloat16)
    )
    return (normed, peak + jnp.log(total))


def combine(prefix_normed, prefix_lse, own):
    own_out, own_peak, own_total = own
    top = jnp.maximum(prefix_lse, own_peak)
    scale_first = jnp.exp(prefix_lse - top)
    scale_second = jnp.exp(own_peak - top)
    divisor = scale_first + own_total * scale_second
    shape = own_peak.shape + (-1,)
    mixed = (
        prefix_normed.astype(jnp.float32).reshape(shape) * scale_first[..., None]
        + own_out.reshape(shape) * scale_second[..., None]
    )
    mixed = mixed / divisor[..., None]
    return mixed.reshape(own_peak.shape[:-1] + (-1,)).astype(jnp.bfloat16)


def shards(
    inputs,
    norm_gain,
    w_query,
    w_key,
    w_value,
    query_bias,
    key_bias,
    value_bias,
    key_cache,
    value_cache,
    source_doc,
    prefix_len,
):
    full_rows = lax.all_gather(inputs, "corpus", axis=1, tiled=True)
    normed = normalize(full_rows, norm_gain)
    query_lin = jnp.dot(
        normed,
        lax.all_gather(w_query, "fsdp", axis=0, tiled=True),
        preferred_element_type=jnp.float32,
    )
    key_lin = jnp.dot(
        normed,
        lax.all_gather(w_key, "fsdp", axis=0, tiled=True),
        preferred_element_type=jnp.float32,
    )
    value_lin = jnp.dot(
        normed,
        lax.all_gather(w_value, "fsdp", axis=0, tiled=True),
        preferred_element_type=jnp.float32,
    )
    suffixes = source_doc.shape[0]
    width = HD
    q_heads = w_query.shape[1] // width
    kv_heads = w_key.shape[1] // width
    position = prefix_len[:, None] + jnp.arange(SL, dtype=jnp.int32)[None, :]
    cosine, sine = rope_tables(position, width)
    cosine = cosine[:, :, None, :]
    sine = sine[:, :, None, :]
    queries = rotate(
        (query_lin + query_bias).reshape(suffixes, SL, q_heads, width), cosine, sine
    ).astype(jnp.bfloat16)
    own_keys = rotate(
        (key_lin + key_bias).reshape(suffixes, SL, kv_heads, width), cosine, sine
    ).astype(jnp.bfloat16)
    own_keys = own_keys.reshape(suffixes, SL, kv_heads * width)
    own_values = (
        (value_lin + value_bias).astype(jnp.bfloat16).reshape(suffixes, SL, kv_heads * width)
    )
    causal = jnp.arange(SL, dtype=jnp.int32)[None, :] <= jnp.arange(SL, dtype=jnp.int32)[:, None]
    own_part = jax.vmap(partial_attend, in_axes=(0, 0, 0, None))(
        queries, own_keys, own_values, causal
    )
    documents = lax.axis_size("fsdp")
    slots = documents * CAP
    doc_length = key_cache.shape[1]
    order = jnp.arange(suffixes, dtype=jnp.int32)
    earlier = (source_doc[None, :] == source_doc[:, None]) & (order[None, :] < order[:, None])
    ranking = jnp.sum(earlier.astype(jnp.int32), axis=1)
    slot_of = source_doc * CAP + ranking
    matches = slot_of[None, :] == jnp.arange(slots, dtype=jnp.int32)[:, None]
    holder = jnp.sum(jnp.where(matches, order[None, :], 0), axis=1)
    occupied = jnp.any(matches, axis=1)
    slot_length = jnp.where(occupied, jnp.take(prefix_len, holder, axis=0), 0)
    slot_mask = (jnp.arange(doc_length, dtype=jnp.int32)[None, :] < slot_length[:, None]).astype(
        jnp.bfloat16
    )
    slot_queries = jnp.take(queries, holder, axis=0)
    initial = (
        jnp.zeros((suffixes, SL, q_heads * width), jnp.float32),
        jnp.zeros((suffixes, SL, q_heads), jnp.float32),
        jnp.zeros((suffixes, SL, q_heads), jnp.float32),
    )
    key_piece = lax.all_gather(key_cache, "fsdp", axis=0, tiled=True)
    value_piece = lax.all_gather(value_cache, "fsdp", axis=0, tiled=True)
    count = key_piece.shape[0]

    def one_document(item):
        doc_queries, doc_masks, doc_keys, doc_values = item
        live = jnp.broadcast_to(doc_masks[:, None, :] > 0, (CAP, SL, doc_masks.shape[-1]))
        return jax.vmap(partial_attend, in_axes=(0, None, None, 0))(
            doc_queries, doc_keys, doc_values, live
        )

    results = lax.map(
        one_document,
        (
            slot_queries.reshape((count, CAP) + slot_queries.shape[1:]),
            slot_mask.reshape(count, CAP, doc_length),
            key_piece,
            value_piece,
        ),
    )
    results = tuple((part.reshape((count * CAP,) + part.shape[2:]) for part in results))
    inside = (slot_of >= 0) & (slot_of < count * CAP)
    chosen = jnp.clip(slot_of, 0, count * CAP - 1)
    gathered_part = tuple(
        (
            jnp.where(inside[:, None, None], jnp.take(fresh, chosen, axis=0), older)
            for older, fresh in zip(initial, results)
        )
    )
    prefix_normed, prefix_lse = settle(gathered_part)
    attention = combine(prefix_normed, prefix_lse, own_part)
    return attention.reshape(suffixes * SL, q_heads * width)


def solution(mesh):
    in_specs = (
        P("fsdp", "corpus"),
        P(),
        P("fsdp", "corpus"),
        P("fsdp", "corpus"),
        P("fsdp", "corpus"),
        P("corpus"),
        P("corpus"),
        P("corpus"),
        P("fsdp", None, "corpus"),
        P("fsdp", None, "corpus"),
        P("fsdp"),
        P("fsdp"),
    )
    out_specs = P("fsdp", "corpus")
    return jax.shard_map(shards, mesh=mesh, in_specs=in_specs, out_specs=out_specs, check_vma=False)
```

profile of v0, /device:TPU:0, one launch (start us, length us, event | category | flops | bytes accessed | tf_op | source)
XLA Modules:
  0.0 685.7 jit_solution(6007420988527938023)
XLA Ops:
  15.4 31.9 %all-gather.11.cloned.1.call-done = bf16[256,4096]{1,0:T(8,128)(2,1)} async-done(((bf16[256,1024]{1,0:T(8,128)(2,1)}), bf16[256,4096]{1,0:T(8,128)(2,1)}) %all-gather.11.cloned.1.call-update) | async-done | bytes 2097168 | tf_op jit(solution)/shard_map/all_gather | solution.py:97
  49.5 28.5 %all-gather.15.cloned.1.call-done = bf16[4096,256]{1,0:T(8,128)(2,1)} async-done(((bf16[512,256]{1,0:T(8,128)(2,1)}), bf16[4096,256]{1,0:T(8,128)(2,1)}) %all-gather.15.cloned.1.call-update) | async-done | bytes 2097168 | tf_op jit(solution)/shard_map/all_gather | solution.py:106
  80.5 27.7 %all-gather.17.cloned.1.call-done = bf16[4096,256]{1,0:T(8,128)(2,1)} async-done(((bf16[512,256]{1,0:T(8,128)(2,1)}), bf16[4096,256]{1,0:T(8,128)(2,1)}) %all-gather.17.cloned.1.call-update) | async-done | bytes 2097168 | tf_op jit(solution)/shard_map/all_gather | solution.py:111
  110.8 149.5 %all-gather.13.cloned.1.call-done = bf16[4096,2048]{1,0:T(8,128)(2,1)} async-done(((bf16[512,2048]{1,0:T(8,128)(2,1)}), bf16[4096,2048]{1,0:T(8,128)(2,1)}) %all-gather.13.cloned.1.call-update) | async-done | bytes 16777232 | tf_op jit(solution)/shard_map/all_gather | solution.py:101
  260.3 8.2 %fusion.26 = f32[32,8,16,128]{3,1,2,0:T(8,128)S(1)} fusion(bf16[4096,2048]{1,0:T(8,128)(2,1)} %all-gather.13.cloned.1.call-done, f32[2048]{0:T(1024)S(1)} %copy-done.18, bf16[256,4096]{1,0:T(8,128)(2,1)S(1)} %copy-done.7, f32[4096]{0:T(1024)S(1)} %copy-done.17, f32[256]{0:T(256)S(1)} %add_rsqrt_fusion), kind=kOutput, calls=%fused_computation.52 | convolution fusion | flops 4299685888 | bytes 20997120 | tf_op jit(solution)/shard_map/dot_general | solution.py:99
  291.7 50.4 %all-gather.9.cloned.1.call-done = bf16[8,2048,256]{2,1,0:T(8,128)(2,1)} async-done(((bf16[1,2048,256]{2,1,0:T(8,128)(2,1)}), bf16[8,2048,256]{2,1,0:T(8,128)(2,1)}) %all-gather.9.cloned.1.call-update) | async-done | bytes 8388624 | tf_op jit(solution)/shard_map/all_gather | solution.py:156
  342.1 82.1 %all-gather.7.cloned.1.call-done = bf16[8,2048,256]{2,1,0:T(8,128)(2,1)} async-done(((bf16[1,2048,256]{2,1,0:T(8,128)(2,1)}), bf16[8,2048,256]{2,1,0:T(8,128)(2,1)}) %all-gather.7.cloned.1.call-update) | async-done | bytes 8388624 | tf_op jit(solution)/shard_map/all_gather | solution.py:157
  424.2 241.4 %while.14 = (s32[]{:T(128)}, f32[8,2,64,2048]{3,2,1,0:T(8,128)}, f32[8,2,64,16]{2,3,1,0:T(8,128)S(1)}, f32[8,2,64,16]{2,3,1,0:T(8,128)S(1)}, bf16[8,2048,256]{2,...) while((s32[]{:T(128)}, f32[8,2,64,2048]{3,2,1,0:T(8,128)}, ...), condition=%wide.region_7.8_spmd, body=%wide.region_4.0_spmd.sunk | while | flops 2193620992 | bytes 74047632 | solution.py:167
  429.9 7.1 %fusion.71 = (f32[2,64,2,8]{1,3,0,2:T(8,128)S(1)}, f32[2,2048,2,64,8]{1,3,4,2,0:T(8,128)}) fusion(pred[2,2048]{1,0:T(4,128)(4,1)S(1)} %compare_bitcast_fusion.2, bf16[2048,2,128,1,1]{0,2,4,3,1:T(8,128)(2,1)S(1)} %bitcast.138, bf16[2,64,2,8,128]{4,3,2,1,0:T(8,128)(2,1)S(1)} %dynamic-slice_bitcast_fusion.2), kind=kOutput, calls=%fused_computation.9.clone.1 | convolution fusion | flops 1086322688 | bytes 18362368 | tf_op jit(solution)/shard_map/while/body/eval_jaxpr/vmap(tkgd,lkd->tkgl)/dot_general | solution.py:42
  437.1 7.6 %fusion.72 = f32[2,64,2,8,128]{4,1,3,0,2:T(8,128)S(1)} fusion(bf16[2048,2,128,1,1]{0,2,4,3,1:T(8,128)(2,1)S(1)} %bitcast.142, f32[2,2048,2,64,8]{1,3,4,2,0:T(8,128)} %get-tuple-element.168, f32[2,64,2,8]{1,3,0,2:T(8,128)S(1)} %get-tuple-element.169, pred[2,2048]{1,0:T(4,128)(4,1)S(1)} %compare_bitcast_fusion.2), kind=kOutput, calls=%fused_computation.12.clone.1 | convolution fusion | flops 1090519040 | bytes 18886656 | tf_op jit(solution)/shard_map/while/body/eval_jaxpr/vmap(tkgl,lkd->tkgd)/dot_general | solution.py:51
  444.6 7.8 %fusion.73 = f32[2,64,2,8]{1,3,0,2:T(8,128)S(1)} fusion(f32[2,2048,2,64,8]{1,3,4,2,0:T(8,128)} %get-tuple-element.168, f32[2,64,2,8]{1,3,0,2:T(8,128)S(1)} %get-tuple-element.169, pred[2,2048]{1,0:T(4,128)(4,1)S(1)} %compare_bitcast_fusion.2), kind=kLoop, calls=%fused_computation.7.clone.1 | loop fusion | flops 16775168 | bytes 16797696 | tf_op jit(solution)/shard_map/while/body/eval_jaxpr/vmap()/reduce_sum | solution.py:48
  460.1 7.1 %fusion.71 = (f32[2,64,2,8]{1,3,0,2:T(8,128)S(1)}, f32[2,2048,2,64,8]{1,3,4,2,0:T(8,128)}) fusion(pred[2,2048]{1,0:T(4,128)(4,1)S(1)} %compare_bitcast_fusion.2, bf16[2048,2,128,1,1]{0,2,4,3,1:T(8,128)(2,1)S(1)} %bitcast.138, bf16[2,64,2,8,128]{4,3,2,1,0:T(8,128)(2,1)S(1)} %dynamic-slice_bitcast_fusion.2), kind=kOutput, calls=%fused_computation.9.clone.1 | convolution fusion | flops 1086322688 | bytes 18362368 | tf_op jit(solution)/shard_map/while/body/eval_jaxpr/vmap(tkgd,lkd->tkgl)/dot_general | solution.py:42
  467.2 7.6 %fusion.72 = f32[2,64,2,8,128]{4,1,3,0,2:T(8,128)S(1)} fusion(bf16[2048,2,128,1,1]{0,2,4,3,1:T(8,128)(2,1)S(1)} %bitcast.142, f32[2,2048,2,64,8]{1,3,4,2,0:T(8,128)} %get-tuple-element.168, f32[2,64,2,8]{1,3,0,2:T(8,128)S(1)} %get-tuple-element.169, pred[2,2048]{1,0:T(4,128)(4,1)S(1)} %compare_bitcast_fusion.2), kind=kOutput, calls=%fused_computation.12.clone.1 | convolution fusion | flops 1090519040 | bytes 18886656 | tf_op jit(solution)/shard_map/while/body/eval_jaxpr/vmap(tkgl,lkd->tkgd)/dot_general | solution.py:51
  474.8 7.8 %fusion.73 = f32[2,64,2,8]{1,3,0,2:T(8,128)S(1)} fusion(f32[2,2048,2,64,8]{1,3,4,2,0:T(8,128)} %get-tuple-element.168, f32[2,64,2,8]{1,3,0,2:T(8,128)S(1)} %get-tuple-element.169, pred[2,2048]{1,0:T(4,128)(4,1)S(1)} %compare_bitcast_fusion.2), kind=kLoop, calls=%fused_computation.7.clone.1 | loop fusion | flops 16775168 | bytes 16797696 | tf_op jit(solution)/shard_map/while/body/eval_jaxpr/vmap()/reduce_sum | solution.py:48
  490.3 7.1 %fusion.71 = (f32[2,64,2,8]{1,3,0,2:T(8,128)S(1)}, f32[2,2048,2,64,8]{1,3,4,2,0:T(8,128)}) fusion(pred[2,2048]{1,0:T(4,128)(4,1)S(1)} %compare_bitcast_fusion.2, bf16[2048,2,128,1,1]{0,2,4,3,1:T(8,128)(2,1)S(1)} %bitcast.138, bf16[2,64,2,8,128]{4,3,2,1,0:T(8,128)(2,1)S(1)} %dynamic-slice_bitcast_fusion.2), kind=kOutput, calls=%fused_computation.9.clone.1 | convolution fusion | flops 1086322688 | bytes 18362368 | tf_op jit(solution)/shard_map/while/body/eval_jaxpr/vmap(tkgd,lkd->tkgl)/dot_general | solution.py:42
  497.4 7.6 %fusion.72 = f32[2,64,2,8,128]{4,1,3,0,2:T(8,128)S(1)} fusion(bf16[2048,2,128,1,1]{0,2,4,3,1:T(8,128)(2,1)S(1)} %bitcast.142, f32[2,2048,2,64,8]{1,3,4,2,0:T(8,128)} %get-tuple-element.168, f32[2,64,2,8]{1,3,0,2:T(8,128)S(1)} %get-tuple-element.169, pred[2,2048]{1,0:T(4,128)(4,1)S(1)} %compare_bitcast_fusion.2), kind=kOutput, calls=%fused_computation.12.clone.1 | convolution fusion | flops 1090519040 | bytes 18886656 | tf_op jit(solution)/shard_map/while/body/eval_jaxpr/vmap(tkgl,lkd->tkgd)/dot_general | solution.py:51
  505.0 7.8 %fusion.73 = f32[2,64,2,8]{1,3,0,2:T(8,128)S(1)} fusion(f32[2,2048,2,64,8]{1,3,4,2,0:T(8,128)} %get-tuple-element.168, f32[2,64,2,8]{1,3,0,2:T(8,128)S(1)} %get-tuple-element.169, pred[2,2048]{1,0:T(4,128)(4,1)S(1)} %compare_bitcast_fusion.2), kind=kLoop, calls=%fused_computation.7.clone.1 | loop fusion | flops 16775168 | bytes 16797696 | tf_op jit(solution)/shard_map/while/body/eval_jaxpr/vmap()/reduce_sum | solution.py:48
  520.4 7.1 %fusion.71 = (f32[2,64,2,8]{1,3,0,2:T(8,128)S(1)}, f32[2,2048,2,64,8]{1,3,4,2,0:T(8,128)}) fusion(pred[2,2048]{1,0:T(4,128)(4,1)S(1)} %compare_bitcast_fusion.2, bf16[2048,2,128,1,1]{0,2,4,3,1:T(8,128)(2,1)S(1)} %bitcast.138, bf16[2,64,2,8,128]{4,3,2,1,0:T(8,128)(2,1)S(1)} %dynamic-slice_bitcast_fusion.2), kind=kOutput, calls=%fused_computation.9.clone.1 | convolution fusion | flops 1086322688 | bytes 18362368 | tf_op jit(solution)/shard_map/while/body/eval_jaxpr/vmap(tkgd,lkd->tkgl)/dot_general | solution.py:42
  527.6 7.6 %fusion.72 = f32[2,64,2,8,128]{4,1,3,0,2:T(8,128)S(1)} fusion(bf16[2048,2,128,1,1]{0,2,4,3,1:T(8,128)(2,1)S(1)} %bitcast.142, f32[2,2048,2,64,8]{1,3,4,2,0:T(8,128)} %get-tuple-element.168, f32[2,64,2,8]{1,3,0,2:T(8,128)S(1)} %get-tuple-element.169, pred[2,2048]{1,0:T(4,128)(4,1)S(1)} %compare_bitcast_fusion.2), kind=kOutput, calls=%fused_computation.12.clone.1 | convolution fusion | flops 1090519040 | bytes 18886656 | tf_op jit(solution)/shard_map/while/body/eval_jaxpr/vmap(tkgl,lkd->tkgd)/dot_general | solution.py:51
  535.1 7.8 %fusion.73 = f32[2,64,2,8]{1,3,0,2:T(8,128)S(1)} fusion(f32[2,2048,2,64,8]{1,3,4,2,0:T(8,128)} %get-tuple-element.168, f32[2,64,2,8]{1,3,0,2:T(8,128)S(1)} %get-tuple-element.169, pred[2,2048]{1,0:T(4,128)(4,1)S(1)} %compare_bitcast_fusion.2), kind=kLoop, calls=%fused_computation.7.clone.1 | loop fusion | flops 16775168 | bytes 16797696 | tf_op jit(solution)/shard_map/while/body/eval_jaxpr/vmap()/reduce_sum | solution.py:48
  550.6 7.1 %fusion.71 = (f32[2,64,2,8]{1,3,0,2:T(8,128)S(1)}, f32[2,2048,2,64,8]{1,3,4,2,0:T(8,128)}) fusion(pred[2,2048]{1,0:T(4,128)(4,1)S(1)} %compare_bitcast_fusion.2, bf16[2048,2,128,1,1]{0,2,4,3,1:T(8,128)(2,1)S(1)} %bitcast.138, bf16[2,64,2,8,128]{4,3,2,1,0:T(8,128)(2,1)S(1)} %dynamic-slice_bitcast_fusion.2), kind=kOutput, calls=%fused_computation.9.clone.1 | convolution fusion | flops 1086322688 | bytes 18362368 | tf_op jit(solution)/shard_map/while/body/eval_jaxpr/vmap(tkgd,lkd->tkgl)/dot_general | solution.py:42
  557.7 7.6 %fusion.72 = f32[2,64,2,8,128]{4,1,3,0,2:T(8,128)S(1)} fusion(bf16[2048,2,128,1,1]{0,2,4,3,1:T(8,128)(2,1)S(1)} %bitcast.142, f32[2,2048,2,64,8]{1,3,4,2,0:T(8,128)} %get-tuple-element.168, f32[2,64,2,8]{1,3,0,2:T(8,128)S(1)} %get-tuple-element.169, pred[2,2048]{1,0:T(4,128)(4,1)S(1)} %compare_bitcast_fusion.2), kind=kOutput, calls=%fused_computation.12.clone.1 | convolution fusion | flops 1090519040 | bytes 18886656 | tf_op jit(solution)/shard_map/while/body/eval_jaxpr/vmap(tkgl,lkd->tkgd)/dot_general | solution.py:51
  565.3 7.8 %fusion.73 = f32[2,64,2,8]{1,3,0,2:T(8,128)S(1)} fusion(f32[2,2048,2,64,8]{1,3,4,2,0:T(8,128)} %get-tuple-element.168, f32[2,64,2,8]{1,3,0,2:T(8,128)S(1)} %get-tuple-element.169, pred[2,2048]{1,0:T(4,128)(4,1)S(1)} %compare_bitcast_fusion.2), kind=kLoop, calls=%fused_computation.7.clone.1 | loop fusion | flops 16775168 | bytes 16797696 | tf_op jit(solution)/shard_map/while/body/eval_jaxpr/vmap()/reduce_sum | solution.py:48
  580.8 7.1 %fusion.71 = (f32[2,64,2,8]{1,3,0,2:T(8,128)S(1)}, f32[2,2048,2,64,8]{1,3,4,2,0:T(8,128)}) fusion(pred[2,2048]{1,0:T(4,128)(4,1)S(1)} %compare_bitcast_fusion.2, bf16[2048,2,128,1,1]{0,2,4,3,1:T(8,128)(2,1)S(1)} %bitcast.138, bf16[2,64,2,8,128]{4,3,2,1,0:T(8,128)(2,1)S(1)} %dynamic-slice_bitcast_fusion.2), kind=kOutput, calls=%fused_computation.9.clone.1 | convolution fusion | flops 1086322688 | bytes 18362368 | tf_op jit(solution)/shard_map/while/body/eval_jaxpr/vmap(tkgd,lkd->tkgl)/dot_general | solution.py:42
  587.9 7.6 %fusion.72 = f32[2,64,2,8,128]{4,1,3,0,2:T(8,128)S(1)} fusion(bf16[2048,2,128,1,1]{0,2,4,3,1:T(8,128)(2,1)S(1)} %bitcast.142, f32[2,2048,2,64,8]{1,3,4,2,0:T(8,128)} %get-tuple-element.168, f32[2,64,2,8]{1,3,0,2:T(8,128)S(1)} %get-tuple-element.169, pred[2,2048]{1,0:T(4,128)(4,1)S(1)} %compare_bitcast_fusion.2), kind=kOutput, calls=%fused_computation.12.clone.1 | convolution fusion | flops 1090519040 | bytes 18886656 | tf_op jit(solution)/shard_map/while/body/eval_jaxpr/vmap(tkgl,lkd->tkgd)/dot_general | solution.py:51
  595.5 7.8 %fusion.73 = f32[2,64,2,8]{1,3,0,2:T(8,128)S(1)} fusion(f32[2,2048,2,64,8]{1,3,4,2,0:T(8,128)} %get-tuple-element.168, f32[2,64,2,8]{1,3,0,2:T(8,128)S(1)} %get-tuple-element.169, pred[2,2048]{1,0:T(4,128)(4,1)S(1)} %compare_bitcast_fusion.2), kind=kLoop, calls=%fused_computation.7.clone.1 | loop fusion | flops 16775168 | bytes 16797696 | tf_op jit(solution)/shard_map/while/body/eval_jaxpr/vmap()/reduce_sum | solution.py:48
  611.0 7.1 %fusion.71 = (f32[2,64,2,8]{1,3,0,2:T(8,128)S(1)}, f32[2,2048,2,64,8]{1,3,4,2,0:T(8,128)}) fusion(pred[2,2048]{1,0:T(4,128)(4,1)S(1)} %compare_bitcast_fusion.2, bf16[2048,2,128,1,1]{0,2,4,3,1:T(8,128)(2,1)S(1)} %bitcast.138, bf16[2,64,2,8,128]{4,3,2,1,0:T(8,128)(2,1)S(1)} %dynamic-slice_bitcast_fusion.2), kind=kOutput, calls=%fused_computation.9.clone.1 | convolution fusion | flops 1086322688 | bytes 18362368 | tf_op jit(solution)/shard_map/while/body/eval_jaxpr/vmap(tkgd,lkd->tkgl)/dot_general | solution.py:42
  618.1 7.6 %fusion.72 = f32[2,64,2,8,128]{4,1,3,0,2:T(8,128)S(1)} fusion(bf16[2048,2,128,1,1]{0,2,4,3,1:T(8,128)(2,1)S(1)} %bitcast.142, f32[2,2048,2,64,8]{1,3,4,2,0:T(8,128)} %get-tuple-element.168, f32[2,64,2,8]{1,3,0,2:T(8,128)S(1)} %get-tuple-element.169, pred[2,2048]{1,0:T(4,128)(4,1)S(1)} %compare_bitcast_fusion.2), kind=kOutput, calls=%fused_computation.12.clone.1 | convolution fusion | flops 1090519040 | bytes 18886656 | tf_op jit(solution)/shard_map/while/body/eval_jaxpr/vmap(tkgl,lkd->tkgd)/dot_general | solution.py:51
  625.7 7.8 %fusion.73 = f32[2,64,2,8]{1,3,0,2:T(8,128)S(1)} fusion(f32[2,2048,2,64,8]{1,3,4,2,0:T(8,128)} %get-tuple-element.168, f32[2,64,2,8]{1,3,0,2:T(8,128)S(1)} %get-tuple-element.169, pred[2,2048]{1,0:T(4,128)(4,1)S(1)} %compare_bitcast_fusion.2), kind=kLoop, calls=%fused_computation.7.clone.1 | loop fusion | flops 16775168 | bytes 16797696 | tf_op jit(solution)/shard_map/while/body/eval_jaxpr/vmap()/reduce_sum | solution.py:48
  641.1 7.1 %fusion.71 = (f32[2,64,2,8]{1,3,0,2:T(8,128)S(1)}, f32[2,2048,2,64,8]{1,3,4,2,0:T(8,128)}) fusion(pred[2,2048]{1,0:T(4,128)(4,1)S(1)} %compare_bitcast_fusion.2, bf16[2048,2,128,1,1]{0,2,4,3,1:T(8,128)(2,1)S(1)} %bitcast.138, bf16[2,64,2,8,128]{4,3,2,1,0:T(8,128)(2,1)S(1)} %dynamic-slice_bitcast_fusion.2), kind=kOutput, calls=%fused_computation.9.clone.1 | convolution fusion | flops 1086322688 | bytes 18362368 | tf_op jit(solution)/shard_map/while/body/eval_jaxpr/vmap(tkgd,lkd->tkgl)/dot_general | solution.py:42
  648.2 7.6 %fusion.72 = f32[2,64,2,8,128]{4,1,3,0,2:T(8,128)S(1)} fusion(bf16[2048,2,128,1,1]{0,2,4,3,1:T(8,128)(2,1)S(1)} %bitcast.142, f32[2,2048,2,64,8]{1,3,4,2,0:T(8,128)} %get-tuple-element.168, f32[2,64,2,8]{1,3,0,2:T(8,128)S(1)} %get-tuple-element.169, pred[2,2048]{1,0:T(4,128)(4,1)S(1)} %compare_bitcast_fusion.2), kind=kOutput, calls=%fused_computation.12.clone.1 | convolution fusion | flops 1090519040 | bytes 18886656 | tf_op jit(solution)/shard_map/while/body/eval_jaxpr/vmap(tkgl,lkd->tkgd)/dot_general | solution.py:51
  655.8 7.8 %fusion.73 = f32[2,64,2,8]{1,3,0,2:T(8,128)S(1)} fusion(f32[2,2048,2,64,8]{1,3,4,2,0:T(8,128)} %get-tuple-element.168, f32[2,64,2,8]{1,3,0,2:T(8,128)S(1)} %get-tuple-element.169, pred[2,2048]{1,0:T(4,128)(4,1)S(1)} %compare_bitcast_fusion.2), kind=kLoop, calls=%fused_computation.7.clone.1 | loop fusion | flops 16775168 | bytes 16797696 | tf_op jit(solution)/shard_map/while/body/eval_jaxpr/vmap()/reduce_sum | solution.py:48
  (207 shorter events, 113.2 us)
Async XLA Ops:
  6.5 40.7 %all-gather.11.cloned.1.call-start = ((), (), s32[]{:S(2)}) async-start(), calls=%async_computation.2 | async-start | bytes 2621440 | tf_op jit(solution)/shard_map/all_gather | solution.py:97
  7.3 70.7 %all-gather.15.cloned.1.call-start = ((), (), s32[]{:S(2)}) async-start(), calls=%async_computation.4 | async-start | bytes 2359296 | tf_op jit(solution)/shard_map/all_gather | solution.py:106
  8.0 100.2 %all-gather.17.cloned.1.call-start = ((), (), s32[]{:S(2)}) async-start(), calls=%async_computation.5 | async-start | bytes 2359296 | tf_op jit(solution)/shard_map/all_gather | solution.py:111
  8.7 1.8 copy-start.16
  8.8 4.3 copy-start
  8.8 251.5 %all-gather.13.cloned.1.call-start = ((), (), s32[]{:S(2)}) async-start(), calls=%async_computation.3 | async-start | bytes 18874368 | tf_op jit(solution)/shard_map/all_gather | solution.py:101
  9.3 332.7 %all-gather.9.cloned.1.call-start = ((), (), s32[]{:S(2)}) async-start(), calls=%async_computation.1 | async-start | bytes 9437184 | tf_op jit(solution)/shard_map/all_gather | solution.py:156
  9.9 68.1 %copy-start.17 = (f32[4096]{0:T(1024)S(1)}, f32[4096]{0:T(1024)}, u32[]{:S(2)}) copy-start(f32[4096]{0:T(1024)} %param.17) | copy-start | bytes 49156
  9.9 68.1 %copy-start.19 = (f32[256]{0:T(256)S(1)}, f32[256]{0:T(256)}, u32[]{:S(2)}) copy-start(f32[256]{0:T(256)} %param.22) | copy-start | bytes 3076
  9.9 414.2 %all-gather.7.cloned.1.call-start = ((), (), s32[]{:S(2)}) async-start(), calls=%async_computation | async-start | bytes 9437184 | tf_op jit(solution)/shard_map/all_gather | solution.py:157
  12.2 3.2 copy-start.14
  47.3 30.7 %copy-start.7 = (bf16[256,4096]{1,0:T(8,128)(2,1)S(1)}, bf16[256,4096]{1,0:T(8,128)(2,1)}, u32[]{:S(2)}) copy-start(bf16[256,4096]{1,0:T(8,128)(2,1)} %all-gather.11.cloned.1.call-done) | copy-start | bytes 6291460
  49.5 58.7 %copy-start.20 = (f32[256]{0:T(256)S(1)}, f32[256]{0:T(256)}, u32[]{:S(2)}) copy-start(f32[256]{0:T(256)} %param.23) | copy-start | bytes 3076
  80.5 179.8 %copy-start.18 = (f32[2048]{0:T(1024)S(1)}, f32[2048]{0:T(1024)}, u32[]{:S(2)}) copy-start(f32[2048]{0:T(1024)} %param.21) | copy-start | bytes 24580
  269.6 2.0 copy-start.5
  273.9 1.4 copy-start.2
  283.5 3.0 copy-start.3
  287.0 137.1 %copy-start.8 = (f32[8,2,64,16]{2,3,1,0:T(8,128)S(1)}, f32[8,2,64,16]{2,3,1,0:T(8,128)}, u32[]{:S(2)}) copy-start(f32[8,2,64,16]{2,3,1,0:T(8,128)} %custom-call.12) | copy-start | bytes 196612
  287.0 137.1 %copy-start.9 = (f32[8,2,64,16]{2,3,1,0:T(8,128)S(1)}, f32[8,2,64,16]{2,3,1,0:T(8,128)}, u32[]{:S(2)}) copy-start(f32[8,2,64,16]{2,3,1,0:T(8,128)} %custom-call.11) | copy-start | bytes 196612
  429.9 7.1 %copy-start.1 = (bf16[1,2048,256]{1,2,0:T(8,128)(2,1)S(1)}, bf16[1,2048,256]{1,2,0:T(8,128)(2,1)}, u32[]{:S(2)}) copy-start(bf16[1,2048,256]{1,2,0:T(8,128)(2,1)} %copy.160) | copy-start | bytes 3145732 | tf_op jit(solution)/shard_map/while
  460.1 7.1 %copy-start.1 = (bf16[1,2048,256]{1,2,0:T(8,128)(2,1)S(1)}, bf16[1,2048,256]{1,2,0:T(8,128)(2,1)}, u32[]{:S(2)}) copy-start(bf16[1,2048,256]{1,2,0:T(8,128)(2,1)} %copy.160) | copy-start | bytes 3145732 | tf_op jit(solution)/shard_map/while
  490.3 7.1 %copy-start.1 = (bf16[1,2048,256]{1,2,0:T(8,128)(2,1)S(1)}, bf16[1,2048,256]{1,2,0:T(8,128)(2,1)}, u32[]{:S(2)}) copy-start(bf16[1,2048,256]{1,2,0:T(8,128)(2,1)} %copy.160) | copy-start | bytes 3145732 | tf_op jit(solution)/shard_map/while
  520.4 7.1 %copy-start.1 = (bf16[1,2048,256]{1,2,0:T(8,128)(2,1)S(1)}, bf16[1,2048,256]{1,2,0:T(8,128)(2,1)}, u32[]{:S(2)}) copy-start(bf16[1,2048,256]{1,2,0:T(8,128)(2,1)} %copy.160) | copy-start | bytes 3145732 | tf_op jit(solution)/shard_map/while
  550.6 7.1 %copy-start.1 = (bf16[1,2048,256]{1,2,0:T(8,128)(2,1)S(1)}, bf16[1,2048,256]{1,2,0:T(8,128)(2,1)}, u32[]{:S(2)}) copy-start(bf16[1,2048,256]{1,2,0:T(8,128)(2,1)} %copy.160) | copy-start | bytes 3145732 | tf_op jit(solution)/shard_map/while
  580.8 7.1 %copy-start.1 = (bf16[1,2048,256]{1,2,0:T(8,128)(2,1)S(1)}, bf16[1,2048,256]{1,2,0:T(8,128)(2,1)}, u32[]{:S(2)}) copy-start(bf16[1,2048,256]{1,2,0:T(8,128)(2,1)} %copy.160) | copy-start | bytes 3145732 | tf_op jit(solution)/shard_map/while
  611.0 7.1 %copy-start.1 = (bf16[1,2048,256]{1,2,0:T(8,128)(2,1)S(1)}, bf16[1,2048,256]{1,2,0:T(8,128)(2,1)}, u32[]{:S(2)}) copy-start(bf16[1,2048,256]{1,2,0:T(8,128)(2,1)} %copy.160) | copy-start | bytes 3145732 | tf_op jit(solution)/shard_map/while
  641.1 7.1 %copy-start.1 = (bf16[1,2048,256]{1,2,0:T(8,128)(2,1)S(1)}, bf16[1,2048,256]{1,2,0:T(8,128)(2,1)}, u32[]{:S(2)}) copy-start(bf16[1,2048,256]{1,2,0:T(8,128)(2,1)} %copy.160) | copy-start | bytes 3145732 | tf_op jit(solution)/shard_map/while
  666.2 4.9 copy-start.11
  666.2 4.9 copy-start.15
  672.9 1.6 copy-start.6
  672.9 1.6 copy-start.12
  672.9 1.6 copy-start.13
  (2 other events, 1.8 us)
Sparse Core Ops, SparseCore 0:
  9.2 38.0 all-gather.10
  48.8 29.0 all-gather.14
  79.6 28.5 all-gather.16
  109.7 150.5 all-gather.12
  261.7 80.2 all-gather.8
  343.5 80.5 all-gather.6
where the time goes:
time: 687 us; the launch traced here: 686 us
  waiting for transfers between devices  374 us (54%)
  matrix products  133 us (19%)
  local copies, waits for them, and re-layouts  84.7 us (12%)
  other arithmetic  80.2 us (12%)
  between operations  13.9 us (2%)
    all_gather x1, waiting for transfers between devices, shards(): lax.all_gather(w_query, 'fsdp', axis=0, tiled=True)  150 us
    all_gather x1, waiting for transfers between devices, shards(): value_piece = lax.all_gather(value_cache, 'fsdp', axis=0, tiled=True)  82.1 us
    reduce_sum x9, other arithmetic, partial_attend(): total = jnp.sum(weights, axis=-1)  63 us
    dot_general x9, matrix products, partial_attend(): jnp.einsum('tkgl,lkd->tkgd', rounded, value_rows, preferred_element_type=...  61.1 us
    dot_general x9, matrix products, partial_attend(): jnp.einsum('tkgd,lkd->tkgl', grouped, key_rows, preferred_element_type=jn...  58.6 us
    all_gather x1, waiting for transfers between devices, shards(): key_piece = lax.all_gather(key_cache, 'fsdp', axis=0, tiled=True)  50.4 us
    dynamic_slice x32, local copies, waits for them, and re-layouts, shards(): lax.map(one_document, (slot_queries.reshape((count, CAP) + slot_queries.s...  37.3 us
    all_gather x1, waiting for transfers between devices, shards(): full_rows = lax.all_gather(inputs, 'corpus', axis=1, tiled=True)  31.9 us
  transfers between devices with their start and end apart: 6, of which 6 were waited for; matrix products, arithmetic and copies ran while one was open for 6% of the time, Pallas kernels for 0%

commit v1 on v0

--- a/solution.py
+++ b/solution.py
@@ -153,8 +153,13 @@
         jnp.zeros((suffixes, SL, q_heads), jnp.float32),
         jnp.zeros((suffixes, SL, q_heads), jnp.float32),
     )
-    key_piece = lax.all_gather(key_cache, "fsdp", axis=0, tiled=True)
-    value_piece = lax.all_gather(value_cache, "fsdp", axis=0, tiled=True)
+    key_piece, value_piece = jnp.split(
+        lax.all_gather(
+            jnp.concatenate([key_cache, value_cache], axis=1), "fsdp", axis=0, tiled=True
+        ),
+        [key_cache.shape[1]],
+        axis=1,
+    )
     count = key_piece.shape[0]
 
     def one_document(item):

time: 687 us -> 686 us (level)
  waiting for transfers between devices: 374 us -> 358 us
  local copies, waits for them, and re-layouts: 84.7 us -> 97.1 us
    all_gather x2 -> x1, waiting for transfers between devices: 132 us -> 119 us  [shards(): lax.all_gather(jnp.concatenate([key_cache, value_cache], axis=1), 'fsdp',...]
    split x0 -> x1, local copies, waits for them, and re-layouts: none -> 11.3 us  [shards(): jnp.split(lax.all_gather(jnp.concatenate([key_cache, value_cache], axis=1...]
  transfers between devices with their start and end apart: 6 -> 5, of which waited for: 6 -> 5; matrix products, arithmetic and copies ran while one was open for 6% -> 6% of each run, Pallas kernels for 0% -> 0%
where the time goes in v1:
time: 686 us; the launch traced here: 684 us
  waiting for transfers between devices  358 us (52%)
  matrix products  133 us (19%)
  local copies, waits for them, and re-layouts  97.1 us (14%)
  other arithmetic  81.6 us (12%)
  between operations  13.6 us (2%)
    all_gather x1, waiting for transfers between devices, shards(): lax.all_gather(w_query, 'fsdp', axis=0, tiled=True)  150 us
    all_gather x1, waiting for transfers between devices, shards(): lax.all_gather(jnp.concatenate([key_cache, value_cache], axis=1), 'fsdp',...  119 us
    reduce_sum x9, other arithmetic, partial_attend(): total = jnp.sum(weights, axis=-1)  63 us
    dot_general x9, matrix products, partial_attend(): jnp.einsum('tkgl,lkd->tkgd', rounded, value_rows, preferred_element_type=...  61.1 us
    dot_general x9, matrix products, partial_attend(): jnp.einsum('tkgd,lkd->tkgl', grouped, key_rows, preferred_element_type=jn...  58.7 us
    dynamic_slice x32, local copies, waits for them, and re-layouts, shards(): lax.map(one_document, (slot_queries.reshape((count, CAP) + slot_queries.s...  37.3 us
    all_gather x1, waiting for transfers between devices, shards(): full_rows = lax.all_gather(inputs, 'corpus', axis=1, tiled=True)  30.9 us
    all_gather x1, waiting for transfers between devices, shards(): lax.all_gather(w_key, 'fsdp', axis=0, tiled=True)  28.5 us
  transfers between devices with their start and end apart: 5, of which 5 were waited for; matrix products, arithmetic and copies ran while one was open for 6% of the time, Pallas kernels for 0%

profile of v1, /device:TPU:0, one launch (start us, length us, event | category | flops | bytes accessed | tf_op | source)
XLA Modules:
  0.0 684.0 jit_solution(12089153393720007304)
XLA Ops:
  16.4 30.9 %all-gather.8.cloned.1.call-done = bf16[256,4096]{1,0:T(8,128)(2,1)} async-done(((bf16[256,1024]{1,0:T(8,128)(2,1)}), bf16[256,4096]{1,0:T(8,128)(2,1)}) %all-gather.8.cloned.1.call-update) | async-done | bytes 2097168 | tf_op jit(solution)/shard_map/all_gather | solution.py:97
  49.5 28.5 %all-gather.12.cloned.1.call-done = bf16[4096,256]{1,0:T(8,128)(2,1)} async-done(((bf16[512,256]{1,0:T(8,128)(2,1)}), bf16[4096,256]{1,0:T(8,128)(2,1)}) %all-gather.12.cloned.1.call-update) | async-done | bytes 2097168 | tf_op jit(solution)/shard_map/all_gather | solution.py:106
  80.5 27.7 %all-gather.14.cloned.1.call-done = bf16[4096,256]{1,0:T(8,128)(2,1)} async-done(((bf16[512,256]{1,0:T(8,128)(2,1)}), bf16[4096,256]{1,0:T(8,128)(2,1)}) %all-gather.14.cloned.1.call-update) | async-done | bytes 2097168 | tf_op jit(solution)/shard_map/all_gather | solution.py:111
  110.8 149.5 %all-gather.10.cloned.1.call-done = bf16[4096,2048]{1,0:T(8,128)(2,1)} async-done(((bf16[512,2048]{1,0:T(8,128)(2,1)}), bf16[4096,2048]{1,0:T(8,128)(2,1)}) %all-gather.10.cloned.1.call-update) | async-done | bytes 16777232 | tf_op jit(solution)/shard_map/all_gather | solution.py:101
  260.4 8.2 %fusion.26 = f32[32,8,16,128]{3,1,2,0:T(8,128)S(1)} fusion(bf16[4096,2048]{1,0:T(8,128)(2,1)} %all-gather.10.cloned.1.call-done, f32[2048]{0:T(1024)S(1)} %copy-done.20, bf16[256,4096]{1,0:T(8,128)(2,1)S(1)} %copy-done.7, f32[4096]{0:T(1024)S(1)} %copy-done.19, f32[256]{0:T(256)S(1)} %add_rsqrt_fusion), kind=kOutput, calls=%fused_computation.53 | convolution fusion | flops 4299685888 | bytes 20997120 | tf_op jit(solution)/shard_map/dot_general | solution.py:99
  292.1 119.1 %all-gather.6.cloned.1.call-done = bf16[8,4096,256]{2,1,0:T(8,128)(2,1)} async-done(((bf16[1,4096,256]{2,1,0:T(8,128)(2,1)}), bf16[8,4096,256]{2,1,0:T(8,128)(2,1)}) %all-gather.6.cloned.1.call-update) | async-done | bytes 16777232 | tf_op jit(solution)/shard_map/all_gather | solution.py:157
  411.2 11.3 %fusion.56 = (bf16[8,2048,256]{2,1,0:T(8,128)(2,1)}, bf16[8,2048,256]{2,1,0:T(8,128)(2,1)}) fusion(bf16[8,4096,256]{2,1,0:T(8,128)(2,1)} %all-gather.6.cloned.1.call-done), kind=kLoop, calls=%fused_computation.106 | loop fusion | bytes 33554432 | tf_op jit(solution)/shard_map/split | solution.py:156
  422.5 241.6 %while.14 = (s32[]{:T(128)}, f32[8,2,64,2048]{3,2,1,0:T(8,128)}, f32[8,2,64,16]{2,3,1,0:T(8,128)S(1)}, f32[8,2,64,16]{2,3,1,0:T(8,128)S(1)}, bf16[8,2048,256]{2,...) while((s32[]{:T(128)}, f32[8,2,64,2048]{3,2,1,0:T(8,128)}, ...), condition=%wide.region_7.8_spmd, body=%wide.region_4.0_spmd.sunk | while | flops 2193620992 | bytes 74047632 | solution.py:172
  428.5 7.1 %fusion.72 = (f32[2,64,2,8]{1,3,0,2:T(8,128)S(1)}, f32[2,2048,2,64,8]{1,3,4,2,0:T(8,128)}) fusion(pred[2,2048]{1,0:T(4,128)(4,1)S(1)} %compare_bitcast_fusion.2, bf16[2048,2,128,1,1]{0,2,4,3,1:T(8,128)(2,1)S(1)} %bitcast.138, bf16[2,64,2,8,128]{4,3,2,1,0:T(8,128)(2,1)S(1)} %dynamic-slice_bitcast_fusion.2), kind=kOutput, calls=%fused_computation.9.clone.1 | convolution fusion | flops 1086322688 | bytes 18362368 | tf_op jit(solution)/shard_map/while/body/eval_jaxpr/vmap(tkgd,lkd->tkgl)/dot_general | solution.py:42
  435.7 7.6 %fusion.73 = f32[2,64,2,8,128]{4,1,3,0,2:T(8,128)S(1)} fusion(bf16[2048,2,128,1,1]{0,2,4,3,1:T(8,128)(2,1)S(1)} %bitcast.142, f32[2,2048,2,64,8]{1,3,4,2,0:T(8,128)} %get-tuple-element.170, f32[2,64,2,8]{1,3,0,2:T(8,128)S(1)} %get-tuple-element.171, pred[2,2048]{1,0:T(4,128)(4,1)S(1)} %compare_bitcast_fusion.2), kind=kOutput, calls=%fused_computation.12.clone.1 | convolution fusion | flops 1090519040 | bytes 18886656 | tf_op jit(solution)/shard_map/while/body/eval_jaxpr/vmap(tkgl,lkd->tkgd)/dot_general | solution.py:51
  443.2 7.8 %fusion.74 = f32[2,64,2,8]{1,3,0,2:T(8,128)S(1)} fusion(f32[2,2048,2,64,8]{1,3,4,2,0:T(8,128)} %get-tuple-element.170, f32[2,64,2,8]{1,3,0,2:T(8,128)S(1)} %get-tuple-element.171, pred[2,2048]{1,0:T(4,128)(4,1)S(1)} %compare_bitcast_fusion.2), kind=kLoop, calls=%fused_computation.7.clone.1 | loop fusion | flops 16775168 | bytes 16797696 | tf_op jit(solution)/shard_map/while/body/eval_jaxpr/vmap()/reduce_sum | solution.py:48
  458.7 7.1 %fusion.72 = (f32[2,64,2,8]{1,3,0,2:T(8,128)S(1)}, f32[2,2048,2,64,8]{1,3,4,2,0:T(8,128)}) fusion(pred[2,2048]{1,0:T(4,128)(4,1)S(1)} %compare_bitcast_fusion.2, bf16[2048,2,128,1,1]{0,2,4,3,1:T(8,128)(2,1)S(1)} %bitcast.138, bf16[2,64,2,8,128]{4,3,2,1,0:T(8,128)(2,1)S(1)} %dynamic-slice_bitcast_fusion.2), kind=kOutput, calls=%fused_computation.9.clone.1 | convolution fusion | flops 1086322688 | bytes 18362368 | tf_op jit(solution)/shard_map/while/body/eval_jaxpr/vmap(tkgd,lkd->tkgl)/dot_general | solution.py:42
  465.8 7.6 %fusion.73 = f32[2,64,2,8,128]{4,1,3,0,2:T(8,128)S(1)} fusion(bf16[2048,2,128,1,1]{0,2,4,3,1:T(8,128)(2,1)S(1)} %bitcast.142, f32[2,2048,2,64,8]{1,3,4,2,0:T(8,128)} %get-tuple-element.170, f32[2,64,2,8]{1,3,0,2:T(8,128)S(1)} %get-tuple-element.171, pred[2,2048]{1,0:T(4,128)(4,1)S(1)} %compare_bitcast_fusion.2), kind=kOutput, calls=%fused_computation.12.clone.1 | convolution fusion | flops 1090519040 | bytes 18886656 | tf_op jit(solution)/shard_map/while/body/eval_jaxpr/vmap(tkgl,lkd->tkgd)/dot_general | solution.py:51
  473.4 7.8 %fusion.74 = f32[2,64,2,8]{1,3,0,2:T(8,128)S(1)} fusion(f32[2,2048,2,64,8]{1,3,4,2,0:T(8,128)} %get-tuple-element.170, f32[2,64,2,8]{1,3,0,2:T(8,128)S(1)} %get-tuple-element.171, pred[2,2048]{1,0:T(4,128)(4,1)S(1)} %compare_bitcast_fusion.2), kind=kLoop, calls=%fused_computation.7.clone.1 | loop fusion | flops 16775168 | bytes 16797696 | tf_op jit(solution)/shard_map/while/body/eval_jaxpr/vmap()/reduce_sum | solution.py:48
  488.9 7.1 %fusion.72 = (f32[2,64,2,8]{1,3,0,2:T(8,128)S(1)}, f32[2,2048,2,64,8]{1,3,4,2,0:T(8,128)}) fusion(pred[2,2048]{1,0:T(4,128)(4,1)S(1)} %compare_bitcast_fusion.2, bf16[2048,2,128,1,1]{0,2,4,3,1:T(8,128)(2,1)S(1)} %bitcast.138, bf16[2,64,2,8,128]{4,3,2,1,0:T(8,128)(2,1)S(1)} %dynamic-slice_bitcast_fusion.2), kind=kOutput, calls=%fused_computation.9.clone.1 | convolution fusion | flops 1086322688 | bytes 18362368 | tf_op jit(solution)/shard_map/while/body/eval_jaxpr/vmap(tkgd,lkd->tkgl)/dot_general | solution.py:42
  496.0 7.6 %fusion.73 = f32[2,64,2,8,128]{4,1,3,0,2:T(8,128)S(1)} fusion(bf16[2048,2,128,1,1]{0,2,4,3,1:T(8,128)(2,1)S(1)} %bitcast.142, f32[2,2048,2,64,8]{1,3,4,2,0:T(8,128)} %get-tuple-element.170, f32[2,64,2,8]{1,3,0,2:T(8,128)S(1)} %get-tuple-element.171, pred[2,2048]{1,0:T(4,128)(4,1)S(1)} %compare_bitcast_fusion.2), kind=kOutput, calls=%fused_computation.12.clone.1 | convolution fusion | flops 1090519040 | bytes 18886656 | tf_op jit(solution)/shard_map/while/body/eval_jaxpr/vmap(tkgl,lkd->tkgd)/dot_general | solution.py:51
  503.6 7.8 %fusion.74 = f32[2,64,2,8]{1,3,0,2:T(8,128)S(1)} fusion(f32[2,2048,2,64,8]{1,3,4,2,0:T(8,128)} %get-tuple-element.170, f32[2,64,2,8]{1,3,0,2:T(8,128)S(1)} %get-tuple-element.171, pred[2,2048]{1,0:T(4,128)(4,1)S(1)} %compare_bitcast_fusion.2), kind=kLoop, calls=%fused_computation.7.clone.1 | loop fusion | flops 16775168 | bytes 16797696 | tf_op jit(solution)/shard_map/while/body/eval_jaxpr/vmap()/reduce_sum | solution.py:48
  519.0 7.1 %fusion.72 = (f32[2,64,2,8]{1,3,0,2:T(8,128)S(1)}, f32[2,2048,2,64,8]{1,3,4,2,0:T(8,128)}) fusion(pred[2,2048]{1,0:T(4,128)(4,1)S(1)} %compare_bitcast_fusion.2, bf16[2048,2,128,1,1]{0,2,4,3,1:T(8,128)(2,1)S(1)} %bitcast.138, bf16[2,64,2,8,128]{4,3,2,1,0:T(8,128)(2,1)S(1)} %dynamic-slice_bitcast_fusion.2), kind=kOutput, calls=%fused_computation.9.clone.1 | convolution fusion | flops 1086322688 | bytes 18362368 | tf_op jit(solution)/shard_map/while/body/eval_jaxpr/vmap(tkgd,lkd->tkgl)/dot_general | solution.py:42
  526.1 7.6 %fusion.73 = f32[2,64,2,8,128]{4,1,3,0,2:T(8,128)S(1)} fusion(bf16[2048,2,128,1,1]{0,2,4,3,1:T(8,128)(2,1)S(1)} %bitcast.142, f32[2,2048,2,64,8]{1,3,4,2,0:T(8,128)} %get-tuple-element.170, f32[2,64,2,8]{1,3,0,2:T(8,128)S(1)} %get-tuple-element.171, pred[2,2048]{1,0:T(4,128)(4,1)S(1)} %compare_bitcast_fusion.2), kind=kOutput, calls=%fused_computation.12.clone.1 | convolution fusion | flops 1090519040 | bytes 18886656 | tf_op jit(solution)/shard_map/while/body/eval_jaxpr/vmap(tkgl,lkd->tkgd)/dot_general | solution.py:51
  533.7 7.8 %fusion.74 = f32[2,64,2,8]{1,3,0,2:T(8,128)S(1)} fusion(f32[2,2048,2,64,8]{1,3,4,2,0:T(8,128)} %get-tuple-element.170, f32[2,64,2,8]{1,3,0,2:T(8,128)S(1)} %get-tuple-element.171, pred[2,2048]{1,0:T(4,128)(4,1)S(1)} %compare_bitcast_fusion.2), kind=kLoop, calls=%fused_computation.7.clone.1 | loop fusion | flops 16775168 | bytes 16797696 | tf_op jit(solution)/shard_map/while/body/eval_jaxpr/vmap()/reduce_sum | solution.py:48
  549.2 7.1 %fusion.72 = (f32[2,64,2,8]{1,3,0,2:T(8,128)S(1)}, f32[2,2048,2,64,8]{1,3,4,2,0:T(8,128)}) fusion(pred[2,2048]{1,0:T(4,128)(4,1)S(1)} %compare_bitcast_fusion.2, bf16[2048,2,128,1,1]{0,2,4,3,1:T(8,128)(2,1)S(1)} %bitcast.138, bf16[2,64,2,8,128]{4,3,2,1,0:T(8,128)(2,1)S(1)} %dynamic-slice_bitcast_fusion.2), kind=kOutput, calls=%fused_computation.9.clone.1 | convolution fusion | flops 1086322688 | bytes 18362368 | tf_op jit(solution)/shard_map/while/body/eval_jaxpr/vmap(tkgd,lkd->tkgl)/dot_general | solution.py:42
  556.3 7.6 %fusion.73 = f32[2,64,2,8,128]{4,1,3,0,2:T(8,128)S(1)} fusion(bf16[2048,2,128,1,1]{0,2,4,3,1:T(8,128)(2,1)S(1)} %bitcast.142, f32[2,2048,2,64,8]{1,3,4,2,0:T(8,128)} %get-tuple-element.170, f32[2,64,2,8]{1,3,0,2:T(8,128)S(1)} %get-tuple-element.171, pred[2,2048]{1,0:T(4,128)(4,1)S(1)} %compare_bitcast_fusion.2), kind=kOutput, calls=%fused_computation.12.clone.1 | convolution fusion | flops 1090519040 | bytes 18886656 | tf_op jit(solution)/shard_map/while/body/eval_jaxpr/vmap(tkgl,lkd->tkgd)/dot_general | solution.py:51
  563.9 7.8 %fusion.74 = f32[2,64,2,8]{1,3,0,2:T(8,128)S(1)} fusion(f32[2,2048,2,64,8]{1,3,4,2,0:T(8,128)} %get-tuple-element.170, f32[2,64,2,8]{1,3,0,2:T(8,128)S(1)} %get-tuple-element.171, pred[2,2048]{1,0:T(4,128)(4,1)S(1)} %compare_bitcast_fusion.2), kind=kLoop, calls=%fused_computation.7.clone.1 | loop fusion | flops 16775168 | bytes 16797696 | tf_op jit(solution)/shard_map/while/body/eval_jaxpr/vmap()/reduce_sum | solution.py:48
  579.4 7.1 %fusion.72 = (f32[2,64,2,8]{1,3,0,2:T(8,128)S(1)}, f32[2,2048,2,64,8]{1,3,4,2,0:T(8,128)}) fusion(pred[2,2048]{1,0:T(4,128)(4,1)S(1)} %compare_bitcast_fusion.2, bf16[2048,2,128,1,1]{0,2,4,3,1:T(8,128)(2,1)S(1)} %bitcast.138, bf16[2,64,2,8,128]{4,3,2,1,0:T(8,128)(2,1)S(1)} %dynamic-slice_bitcast_fusion.2), kind=kOutput, calls=%fused_computation.9.clone.1 | convolution fusion | flops 1086322688 | bytes 18362368 | tf_op jit(solution)/shard_map/while/body/eval_jaxpr/vmap(tkgd,lkd->tkgl)/dot_general | solution.py:42
  586.5 7.6 %fusion.73 = f32[2,64,2,8,128]{4,1,3,0,2:T(8,128)S(1)} fusion(bf16[2048,2,128,1,1]{0,2,4,3,1:T(8,128)(2,1)S(1)} %bitcast.142, f32[2,2048,2,64,8]{1,3,4,2,0:T(8,128)} %get-tuple-element.170, f32[2,64,2,8]{1,3,0,2:T(8,128)S(1)} %get-tuple-element.171, pred[2,2048]{1,0:T(4,128)(4,1)S(1)} %compare_bitcast_fusion.2), kind=kOutput, calls=%fused_computation.12.clone.1 | convolution fusion | flops 1090519040 | bytes 18886656 | tf_op jit(solution)/shard_map/while/body/eval_jaxpr/vmap(tkgl,lkd->tkgd)/dot_general | solution.py:51
  594.1 7.8 %fusion.74 = f32[2,64,2,8]{1,3,0,2:T(8,128)S(1)} fusion(f32[2,2048,2,64,8]{1,3,4,2,0:T(8,128)} %get-tuple-element.170, f32[2,64,2,8]{1,3,0,2:T(8,128)S(1)} %get-tuple-element.171, pred[2,2048]{1,0:T(4,128)(4,1)S(1)} %compare_bitcast_fusion.2), kind=kLoop, calls=%fused_computation.7.clone.1 | loop fusion | flops 16775168 | bytes 16797696 | tf_op jit(solution)/shard_map/while/body/eval_jaxpr/vmap()/reduce_sum | solution.py:48
  609.6 7.1 %fusion.72 = (f32[2,64,2,8]{1,3,0,2:T(8,128)S(1)}, f32[2,2048,2,64,8]{1,3,4,2,0:T(8,128)}) fusion(pred[2,2048]{1,0:T(4,128)(4,1)S(1)} %compare_bitcast_fusion.2, bf16[2048,2,128,1,1]{0,2,4,3,1:T(8,128)(2,1)S(1)} %bitcast.138, bf16[2,64,2,8,128]{4,3,2,1,0:T(8,128)(2,1)S(1)} %dynamic-slice_bitcast_fusion.2), kind=kOutput, calls=%fused_computation.9.clone.1 | convolution fusion | flops 1086322688 | bytes 18362368 | tf_op jit(solution)/shard_map/while/body/eval_jaxpr/vmap(tkgd,lkd->tkgl)/dot_general | solution.py:42
  616.7 7.6 %fusion.73 = f32[2,64,2,8,128]{4,1,3,0,2:T(8,128)S(1)} fusion(bf16[2048,2,128,1,1]{0,2,4,3,1:T(8,128)(2,1)S(1)} %bitcast.142, f32[2,2048,2,64,8]{1,3,4,2,0:T(8,128)} %get-tuple-element.170, f32[2,64,2,8]{1,3,0,2:T(8,128)S(1)} %get-tuple-element.171, pred[2,2048]{1,0:T(4,128)(4,1)S(1)} %compare_bitcast_fusion.2), kind=kOutput, calls=%fused_computation.12.clone.1 | convolution fusion | flops 1090519040 | bytes 18886656 | tf_op jit(solution)/shard_map/while/body/eval_jaxpr/vmap(tkgl,lkd->tkgd)/dot_general | solution.py:51
  624.3 7.8 %fusion.74 = f32[2,64,2,8]{1,3,0,2:T(8,128)S(1)} fusion(f32[2,2048,2,64,8]{1,3,4,2,0:T(8,128)} %get-tuple-element.170, f32[2,64,2,8]{1,3,0,2:T(8,128)S(1)} %get-tuple-element.171, pred[2,2048]{1,0:T(4,128)(4,1)S(1)} %compare_bitcast_fusion.2), kind=kLoop, calls=%fused_computation.7.clone.1 | loop fusion | flops 16775168 | bytes 16797696 | tf_op jit(solution)/shard_map/while/body/eval_jaxpr/vmap()/reduce_sum | solution.py:48
  639.7 7.1 %fusion.72 = (f32[2,64,2,8]{1,3,0,2:T(8,128)S(1)}, f32[2,2048,2,64,8]{1,3,4,2,0:T(8,128)}) fusion(pred[2,2048]{1,0:T(4,128)(4,1)S(1)} %compare_bitcast_fusion.2, bf16[2048,2,128,1,1]{0,2,4,3,1:T(8,128)(2,1)S(1)} %bitcast.138, bf16[2,64,2,8,128]{4,3,2,1,0:T(8,128)(2,1)S(1)} %dynamic-slice_bitcast_fusion.2), kind=kOutput, calls=%fused_computation.9.clone.1 | convolution fusion | flops 1086322688 | bytes 18362368 | tf_op jit(solution)/shard_map/while/body/eval_jaxpr/vmap(tkgd,lkd->tkgl)/dot_general | solution.py:42
  646.8 7.6 %fusion.73 = f32[2,64,2,8,128]{4,1,3,0,2:T(8,128)S(1)} fusion(bf16[2048,2,128,1,1]{0,2,4,3,1:T(8,128)(2,1)S(1)} %bitcast.142, f32[2,2048,2,64,8]{1,3,4,2,0:T(8,128)} %get-tuple-element.170, f32[2,64,2,8]{1,3,0,2:T(8,128)S(1)} %get-tuple-element.171, pred[2,2048]{1,0:T(4,128)(4,1)S(1)} %compare_bitcast_fusion.2), kind=kOutput, calls=%fused_computation.12.clone.1 | convolution fusion | flops 1090519040 | bytes 18886656 | tf_op jit(solution)/shard_map/while/body/eval_jaxpr/vmap(tkgl,lkd->tkgd)/dot_general | solution.py:51
  654.4 7.8 %fusion.74 = f32[2,64,2,8]{1,3,0,2:T(8,128)S(1)} fusion(f32[2,2048,2,64,8]{1,3,4,2,0:T(8,128)} %get-tuple-element.170, f32[2,64,2,8]{1,3,0,2:T(8,128)S(1)} %get-tuple-element.171, pred[2,2048]{1,0:T(4,128)(4,1)S(1)} %compare_bitcast_fusion.2), kind=kLoop, calls=%fused_computation.7.clone.1 | loop fusion | flops 16775168 | bytes 16797696 | tf_op jit(solution)/shard_map/while/body/eval_jaxpr/vmap()/reduce_sum | solution.py:48
  (210 shorter events, 114.7 us)
Async XLA Ops:
  6.5 2.8 copy-start.8
  6.5 2.8 copy-start.9
  6.5 40.8 %all-gather.8.cloned.1.call-start = ((), (), s32[]{:S(2)}) async-start(), calls=%async_computation.1 | async-start | bytes 2621440 | tf_op jit(solution)/shard_map/all_gather | solution.py:97
  7.3 70.8 %all-gather.12.cloned.1.call-start = ((), (), s32[]{:S(2)}) async-start(), calls=%async_computation.3 | async-start | bytes 2359296 | tf_op jit(solution)/shard_map/all_gather | solution.py:106
  8.0 100.2 %all-gather.14.cloned.1.call-start = ((), (), s32[]{:S(2)}) async-start(), calls=%async_computation.4 | async-start | bytes 2359296 | tf_op jit(solution)/shard_map/all_gather | solution.py:111
  8.7 251.6 %all-gather.10.cloned.1.call-start = ((), (), s32[]{:S(2)}) async-start(), calls=%async_computation.2 | async-start | bytes 18874368 | tf_op jit(solution)/shard_map/all_gather | solution.py:101
  9.3 401.8 %all-gather.6.cloned.1.call-start = ((), (), s32[]{:S(2)}) async-start(), calls=%async_computation | async-start | bytes 18874368 | tf_op jit(solution)/shard_map/all_gather | solution.py:157
  10.9 3.3 copy-start
  10.9 67.1 %copy-start.19 = (f32[4096]{0:T(1024)S(1)}, f32[4096]{0:T(1024)}, u32[]{:S(2)}) copy-start(f32[4096]{0:T(1024)} %param.17) | copy-start | bytes 49156
  10.9 67.1 %copy-start.21 = (f32[256]{0:T(256)S(1)}, f32[256]{0:T(256)}, u32[]{:S(2)}) copy-start(f32[256]{0:T(256)} %param.22) | copy-start | bytes 3076
  13.2 3.2 copy-start.16
  47.3 30.7 %copy-start.7 = (bf16[256,4096]{1,0:T(8,128)(2,1)S(1)}, bf16[256,4096]{1,0:T(8,128)(2,1)}, u32[]{:S(2)}) copy-start(bf16[256,4096]{1,0:T(8,128)(2,1)} %all-gather.8.cloned.1.call-done) | copy-start | bytes 6291460
  49.5 58.7 %copy-start.22 = (f32[256]{0:T(256)S(1)}, f32[256]{0:T(256)}, u32[]{:S(2)}) copy-start(f32[256]{0:T(256)} %param.23) | copy-start | bytes 3076
  80.5 179.8 %copy-start.20 = (f32[2048]{0:T(1024)S(1)}, f32[2048]{0:T(1024)}, u32[]{:S(2)}) copy-start(f32[2048]{0:T(1024)} %param.21) | copy-start | bytes 24580
  269.7 2.3 copy-start.5
  274.4 1.4 copy-start.2
  283.9 3.0 copy-start.3
  292.1 130.4 %copy-start.10 = (f32[8,2,64,16]{2,3,1,0:T(8,128)S(1)}, f32[8,2,64,16]{2,3,1,0:T(8,128)}, u32[]{:S(2)}) copy-start(f32[8,2,64,16]{2,3,1,0:T(8,128)} %custom-call.12) | copy-start | bytes 196612
  292.1 130.4 %copy-start.11 = (f32[8,2,64,16]{2,3,1,0:T(8,128)S(1)}, f32[8,2,64,16]{2,3,1,0:T(8,128)}, u32[]{:S(2)}) copy-start(f32[8,2,64,16]{2,3,1,0:T(8,128)} %custom-call.11) | copy-start | bytes 196612
  428.5 7.1 %copy-start.1 = (bf16[1,2048,256]{1,2,0:T(8,128)(2,1)S(1)}, bf16[1,2048,256]{1,2,0:T(8,128)(2,1)}, u32[]{:S(2)}) copy-start(bf16[1,2048,256]{1,2,0:T(8,128)(2,1)} %copy.160) | copy-start | bytes 3145732 | tf_op jit(solution)/shard_map/while
  458.7 7.1 %copy-start.1 = (bf16[1,2048,256]{1,2,0:T(8,128)(2,1)S(1)}, bf16[1,2048,256]{1,2,0:T(8,128)(2,1)}, u32[]{:S(2)}) copy-start(bf16[1,2048,256]{1,2,0:T(8,128)(2,1)} %copy.160) | copy-start | bytes 3145732 | tf_op jit(solution)/shard_map/while
  488.9 7.1 %copy-start.1 = (bf16[1,2048,256]{1,2,0:T(8,128)(2,1)S(1)}, bf16[1,2048,256]{1,2,0:T(8,128)(2,1)}, u32[]{:S(2)}) copy-start(bf16[1,2048,256]{1,2,0:T(8,128)(2,1)} %copy.160) | copy-start | bytes 3145732 | tf_op jit(solution)/shard_map/while
  519.0 7.1 %copy-start.1 = (bf16[1,2048,256]{1,2,0:T(8,128)(2,1)S(1)}, bf16[1,2048,256]{1,2,0:T(8,128)(2,1)}, u32[]{:S(2)}) copy-start(bf16[1,2048,256]{1,2,0:T(8,128)(2,1)} %copy.160) | copy-start | bytes 3145732 | tf_op jit(solution)/shard_map/while
  549.2 7.1 %copy-start.1 = (bf16[1,2048,256]{1,2,0:T(8,128)(2,1)S(1)}, bf16[1,2048,256]{1,2,0:T(8,128)(2,1)}, u32[]{:S(2)}) copy-start(bf16[1,2048,256]{1,2,0:T(8,128)(2,1)} %copy.160) | copy-start | bytes 3145732 | tf_op jit(solution)/shard_map/while
  579.4 7.1 %copy-start.1 = (bf16[1,2048,256]{1,2,0:T(8,128)(2,1)S(1)}, bf16[1,2048,256]{1,2,0:T(8,128)(2,1)}, u32[]{:S(2)}) copy-start(bf16[1,2048,256]{1,2,0:T(8,128)(2,1)} %copy.160) | copy-start | bytes 3145732 | tf_op jit(solution)/shard_map/while
  609.6 7.1 %copy-start.1 = (bf16[1,2048,256]{1,2,0:T(8,128)(2,1)S(1)}, bf16[1,2048,256]{1,2,0:T(8,128)(2,1)}, u32[]{:S(2)}) copy-start(bf16[1,2048,256]{1,2,0:T(8,128)(2,1)} %copy.160) | copy-start | bytes 3145732 | tf_op jit(solution)/shard_map/while
  639.7 7.1 %copy-start.1 = (bf16[1,2048,256]{1,2,0:T(8,128)(2,1)S(1)}, bf16[1,2048,256]{1,2,0:T(8,128)(2,1)}, u32[]{:S(2)}) copy-start(bf16[1,2048,256]{1,2,0:T(8,128)(2,1)} %copy.160) | copy-start | bytes 3145732 | tf_op jit(solution)/shard_map/while
  664.8 4.9 copy-start.13
  664.8 4.9 copy-start.17
  671.5 1.6 copy-start.6
  671.5 1.6 copy-start.14
  671.5 1.6 copy-start.15
  (3 other events, 2.6 us)
Sparse Core Ops, SparseCore 0:
  9.2 38.0 all-gather.7
  48.9 29.0 all-gather.11
  79.6 28.5 all-gather.13
  109.7 150.5 all-gather.9
  261.8 149.3 all-gather.5
